TPU v7x, 32 devices: a whole 2x2x4 slice. The times are simulated.
32 devices in a mesh: segment: 4 (over z), ctx: 4 (over y, x), tp: 2 (over core).
Axes of the slice: x: 2, y: 2, z: 4, core: 2. Of those that a mesh axis runs over, the one named last changes fastest.
Arguments:
- queries: bfloat16 [4, 512, 8, 640], P('segment', 'ctx', 'tp'), may hold values from -200 to 200
- pairs: bfloat16 [4, 512, 8, 256], P('segment', 'ctx', 'tp'), may hold values from -6 to 6
- out_proj: bfloat16 [4, 8, 640, 5120], P('segment', 'tp'), may hold values from -0.625 to 0.625
- lengths: int32 [4, 4], replicated, may hold values from 1 to 256, 512 in all within a row
Outputs:
- scored: bfloat16 [4, 512, 5120], P('segment', 'ctx', 'tp')
Inputs may be any that keep to these rules, and one draw needn't show every extreme that they name: `lengths`: each row sums to 512; its largest length is exactly 256.
All inputs are finite; a program needn't handle non-finite values.
Results may differ from a plain program's by a relative error of at most 0.014.
Values may be sent and summed in bfloat16 or wider, within the bound.
A program may use at most 64 MiB of HBM per device.

v0:
```python
import math
import jax
import jax.numpy as jnp
from jax import lax
from jax.sharding import PartitionSpec as P


def from_behind(value, axis, by):
    size = lax.axis_size(axis)
    return lax.ppermute(value, axis, [(i, (i + by) % size) for i in range(size)])


def rollout_ids(positions, row_lengths):
    row_ends = jnp.cumsum(row_lengths)
    return jnp.sum((positions[:, None] >= row_ends[None, :]).astype(jnp.int32), axis=1)


def attend(query_shard, pair_shard, row_lengths):
    rows_here = query_shard.shape[1]
    local_heads = pair_shard.shape[2]
    head_dim = pair_shard.shape[3] // 2
    group_size = query_shard.shape[3] // head_dim
    first_pos = lax.axis_index("ctx") * rows_here
    query_pos = first_pos + jnp.arange(rows_here, dtype=jnp.int32)
    query_rollout = rollout_ids(query_pos, row_lengths)
    query_heads = query_shard[0].reshape(rows_here, local_heads, group_size, head_dim)
    score_scale = 1.0 / math.sqrt(head_dim)

    def update(state_in, key_block, key_begin):
        running_max, denom, accum = state_in
        block_len = key_block.shape[0]
        key_pos = key_begin + jnp.arange(block_len, dtype=jnp.int32)
        key_rollout = rollout_ids(key_pos, row_lengths)
        visible = (query_rollout[:, None] == key_rollout[None, :]) & (
            key_pos[None, :] <= query_pos[:, None]
        )
        scores = (
            jnp.einsum(
                "rhgd,khd->hgrk",
                query_heads,
                key_block[:, :, :head_dim],
                preferred_element_type=jnp.float32,
            )
            * score_scale
        )
        scores = jnp.where(visible, scores, -1e30)
        new_max = jnp.maximum(running_max, jnp.max(scores, axis=-1))
        rescale = jnp.exp(running_max - new_max)
        weights = jnp.where(visible, jnp.exp(scores - new_max[..., None]), 0.0)
        denom = denom * rescale + jnp.sum(weights, axis=-1)
        added = jnp.einsum(
            "hgrk,khd->hgrd",
            weights.astype(jnp.bfloat16),
            key_block[:, :, head_dim:],
            preferred_element_type=jnp.float32,
        )
        accum = accum * rescale[..., None] + added
        return (new_max, denom, accum)

    starting = (
        jnp.full((local_heads, group_size, rows_here), -1e30, jnp.float32),
        jnp.zeros((local_heads, group_size, rows_here), jnp.float32),
        jnp.zeros((local_heads, group_size, rows_here, head_dim), jnp.float32),
    )
    shards = lax.all_gather(pair_shard[0], "ctx", axis=0, tiled=True)
    shard_rows = shards.shape[0]
    block_len = math.gcd(shard_rows, 512)

    def one_step(step_index, inner):
        key_block = lax.dynamic_slice_in_dim(shards, step_index * block_len, block_len, 0)
        return update(inner, key_block, step_index * block_len)

    running_max, denom, accum = lax.fori_loop(0, shard_rows // block_len, one_step, starting)
    outputs = accum / denom[..., None]
    outputs = jnp.transpose(outputs, (2, 0, 1, 3)).reshape(
        1, rows_here, local_heads, group_size * head_dim
    )
    return outputs.astype(jnp.bfloat16)


def local(queries, pairs, out_proj, lengths):
    section = lax.axis_index("segment")
    own_result = attend(queries, pairs, lengths[section])
    attended = from_behind(own_result, "segment", -1)
    rows_here = attended.shape[1]
    partial_sum = jnp.dot(
        attended.reshape(rows_here, -1),
        out_proj[0].reshape(-1, out_proj.shape[3]),
        preferred_element_type=jnp.float32,
    )
    shares = lax.psum_scatter(
        partial_sum.astype(jnp.bfloat16), "tp", scatter_dimension=1, tiled=True
    )
    return shares.reshape(1, rows_here, -1)


def solution(mesh):
    return jax.shard_map(
        local,
        mesh=mesh,
        in_specs=(
            P("segment", "ctx", "tp", None),
            P("segment", "ctx", "tp", None),
            P("segment", "tp", None, None),
            P(),
        ),
        out_specs=P("segment", "ctx", "tp"),
        check_vma=False,
    )
```

profile of v0, /device:TPU:0, one launch (start us, length us, event | category | flops | bytes accessed | tf_op | source)
XLA Modules:
  0.0 89.1 jit_solution(15405422814970957084)
XLA Ops:
  6.5 0.0 copy-start
  6.5 0.0 all-gather.3.cloned.1.call-start
  6.5 1.7 %copy.16 = bf16[1,128,4,256]{3,1,2,0:T(8,128)(2,1)} copy(bf16[1,128,4,256]{3,2,1,0:T(4,128)(2,1)} %param.5) | data formatting | bytes 524288 | tf_op args[1]
  8.2 0.0 all-gather.3.cloned.1.call-update
  8.3 0.0 reduce-scatter.2.cloned.1.call-start
  8.3 0.0 copy-done
  8.3 0.2 reduce-window.8
  8.5 1.6 %copy.17 = bf16[1,128,4,640]{1,3,2,0:T(8,128)(2,1)S(1)} copy(bf16[1,128,4,640]{3,2,1,0:T(4,128)(2,1)} %param.4) | data formatting | bytes 1310720 | tf_op args[0]
  10.1 0.1 convert_reduce_fusion
  10.2 0.1 convert_reduce_fusion.1
  10.3 0.1 fusion.24
  10.4 28.0 %all-gather.3.cloned.1.call-done = bf16[1,512,4,256]{3,1,2,0:T(8,128)(2,1)} async-done(((bf16[1,128,4,256]{3,1,2,0:T(8,128)(2,1)}), bf16[1,512,4,256]{3,1,2,0:T(8,128)(2,1)}) %all-gather.3.cloned.1.call-update) | async-done | bytes 1048592 | tf_op jit(solution)/shard_map/all_gather | solution.py:65
  38.4 0.0 copy-start.1
  38.4 2.0 %fusion.8 = (f32[4,5,128]{2,1,0:T(8,128)S(1)}, f32[4,512,128,5]{2,1,3,0:T(8,128)S(1)}) fusion(pred[128,512]{0,1:T(8,128)(4,1)S(1)} %fusion.24, bf16[128,4,5,128]{0,3,2,1:T(8,128)(2,1)S(1)} %bitcast.63, bf16[512,4,256]{2,0,1:T(8,128)(2,1)} %bitcast.65), kind=kOutput, calls=%fused_computation.6 | convolution fusion | flops 339473920 | bytes 6498304 | tf_op jit(solution)/shard_map/while/body/eval_jaxpr/rhgd,khd->hgrk/dot_general | solution.py:38
  40.5 1.3 %fusion.9 = f32[4,5,128]{2,1,0:T(8,128)S(1)} fusion(f32[4,512,128,5]{2,1,3,0:T(8,128)S(1)} %get-tuple-element.26, f32[4,5,128]{2,1,0:T(8,128)S(1)} %get-tuple-element.24, pred[128,512]{0,1:T(8,128)(4,1)S(1)} %fusion.24), kind=kLoop, calls=%fused_computation.7 | loop fusion | flops 6551040 | bytes 5328896 | tf_op jit(solution)/shard_map/while/body/eval_jaxpr/reduce_sum | solution.py:50
  41.8 0.0 copy-done.1
  41.8 1.5 %divide_convert_fusion = bf16[128,4,5,128]{0,3,2,1:T(8,128)(2,1)S(1)} fusion(f32[4,512,128,5]{2,1,3,0:T(8,128)S(1)} %get-tuple-element.26, f32[4,5,128]{2,1,0:T(8,128)S(1)} %get-tuple-element.24, pred[128,512]{0,1:T(8,128)(4,1)S(1)} %fusion.24, f32[128,4,5]{0,2,1:T(8,128)S(1)} %bitcast_add_fusion, f32[128,4,5]{0,2,1:T(8,128)S(1)} %get-tuple-element.23, ...), kind=kOutput, calls=%fused_computation.13 | convolution fusion | flops 343080960 | bytes 6537216 | tf_op jit(solution)/shard_map/while/body/eval_jaxpr/hgrk,khd->hgrd/dot_general | solution.py:51
  43.3 0.3 copy.21
  43.6 3.4 %collective-permute-start = (bf16[1,128,4,640]{3,1,2,0:T(8,128)(2,1)S(1)}, bf16[1,128,4,640]{3,1,2,0:T(8,128)(2,1)S(1)}, u32[]{:S(2)}, u32[]{:S(2)}) collective-permute-start(bf16[1,128,4,640]{3,1,2,0:T(8,128)(2,1)S(1)} %copy.21), channel_id=1, source_target_pairs={{0,24},{8,0},{16,8},{24,16},{1,25},{9,1},{17,9},{25,17},{2,26},{10... | collective-permute-start | bytes 1966088 | tf_op jit(solution)/shard_map/ppermute | solution.py:10
  47.0 13.8 %collective-permute-done = bf16[1,128,4,640]{3,1,2,0:T(8,128)(2,1)S(1)} collective-permute-done((bf16[1,128,4,640]{3,1,2,0:T(8,128)(2,1)S(1)}, bf16[1,128,4,640]{3,1,2,0:T(8,128)(2,1)S(1)}, u32[]{:S(2)}, u32[]{:S(2)}) %collective-permute-start) | collective-permute-done | bytes 655392 | tf_op jit(solution)/shard_map/ppermute | solution.py:10
  60.8 11.7 %fusion.5 = bf16[128,5120]{1,0:T(8,128)(2,1)} fusion(bf16[1,4,640,5120]{3,2,1,0:T(8,128)(2,1)} %param.6, bf16[1,128,4,640]{3,1,2,0:T(8,128)(2,1)S(1)} %collective-permute-done), kind=kOutput, calls=%fused_computation.3 | convolution fusion | flops 3356098560 | bytes 28180480 | tf_op jit(solution)/shard_map/dot_general | solution.py:86
  72.5 0.0 reduce-scatter.2.cloned.1.call-update
  72.6 9.7 %reduce-scatter.2.cloned.1.call-done = bf16[128,2560]{1,0:T(8,128)(2,1)} async-done(((bf16[128,5120]{1,0:T(8,128)(2,1)}), bf16[128,2560]{1,0:T(8,128)(2,1)}) %reduce-scatter.2.cloned.1.call-update) | async-done | bytes 655376 | tf_op jit(solution)/shard_map/reduce_scatter | solution.py:91
  (4 shorter events, 0.0 us)
Async XLA Ops:
  6.5 1.8 %copy-start = (s32[4,4]{1,0:T(4,128)S(1)}, s32[4,4]{1,0:T(4,128)}, u32[]{:S(2)}) copy-start(s32[4,4]{1,0:T(4,128)} %param.7) | copy-start | bytes 196
  6.5 31.9 %all-gather.3.cloned.1.call-start = ((), (), s32[]{:S(2)}) async-start(), calls=%async_computation.2 | async-start | bytes 1310720 | tf_op jit(solution)/shard_map/all_gather | solution.py:65
  8.3 74.0 %reduce-scatter.2.cloned.1.call-start = ((), (), s32[]{:S(2)}) async-start(), calls=%async_computation.1 | async-start | bytes 1966080 | tf_op jit(solution)/shard_map/reduce_scatter | solution.py:91
  38.4 3.3 %copy-start.1 = (bf16[1,512,4,256]{3,1,2,0:T(8,128)(2,1)S(1)}, bf16[1,512,4,256]{3,1,2,0:T(8,128)(2,1)}, u32[]{:S(2)}) copy-start(bf16[1,512,4,256]{3,1,2,0:T(8,128)(2,1)} %all-gather.3.cloned.1.call-done) | copy-start | bytes 3145732
  43.6 17.2 %collective-permute-start = (bf16[1,128,4,640]{3,1,2,0:T(8,128)(2,1)S(1)}, bf16[1,128,4,640]{3,1,2,0:T(8,128)(2,1)S(1)}, u32[]{:S(2)}, u32[]{:S(2)}) collective-permute-start(bf16[1,128,4,640]{3,1,2,0:T(8,128)(2,1)S(1)} %copy.21), channel_id=1, source_target_pairs={{0,24},{8,0},{16,8},{24,16},{1,25},{9,1},{17,9},{25,17},{2,26},{10... | collective-permute-start | bytes 1966088 | tf_op jit(solution)/shard_map/ppermute | solution.py:10
Sparse Core Ops, SparseCore 0:
  9.2 29.2 all-gather.2
  72.7 9.5 reduce-scatter.1
where the time goes:
time: 89.3 us; the launch traced here: 89.1 us
  waiting for transfers between devices  51.6 us (58%)
  matrix products  15.2 us (17%)
  between operations  13.5 us (15%)
  local copies, waits for them, and re-layouts  3.62 us (4%)
  starting transfers between devices  3.43 us (4%)
  other arithmetic  1.76 us (2%)
    all_gather x1, waiting for transfers between devices, attend(): shards = lax.all_gather(pair_shard[0], 'ctx', axis=0, tiled=True)  28 us
    ppermute x1, waiting for transfers between devices, from_behind(): lax.ppermute(value, axis, [(i, (i + by) % size) for i in range(size)])  13.8 us
    dot_general x1, matrix products, local(): jnp.dot(attended.reshape(rows_here, -1), out_proj[0].reshape(-1, out_proj...  11.7 us
    reduce_scatter x1, waiting for transfers between devices, local(): lax.psum_scatter(partial_sum.astype(jnp.bfloat16), 'tp', scatter_dimensio...  9.74 us
    ppermute x1, starting transfers between devices, from_behind(): lax.ppermute(value, axis, [(i, (i + by) % size) for i in range(size)])  3.38 us
    unnamed x6, local copies, waits for them, and re-layouts  3.29 us
    dot_general x1, matrix products, update(): jnp.einsum('rhgd,khd->hgrk', query_heads, key_block[:, :, :head_dim], pre...  2.02 us
  transfers between devices with their start and end apart: 3, of which 3 were waited for; matrix products, arithmetic and copies ran while one was open for 2% of the time, Pallas kernels for 0%

commit v1 on v0

--- a/solution.py
+++ b/solution.py
@@ -62,7 +62,12 @@
         jnp.zeros((local_heads, group_size, rows_here), jnp.float32),
         jnp.zeros((local_heads, group_size, rows_here, head_dim), jnp.float32),
     )
-    shards = lax.all_gather(pair_shard[0], "ctx", axis=0, tiled=True)
+    ring = [pair_shard[0]]
+    for hop in range(3):
+        ring.append(lax.ppermute(ring[-1], "ctx", [(dev, (dev + 1) % 4) for dev in range(4)]))
+    shards = jnp.roll(
+        jnp.concatenate(ring[::-1], axis=0), (lax.axis_index("ctx") + 1) * ring[0].shape[0], axis=0
+    )
     shard_rows = shards.shape[0]
     block_len = math.gcd(shard_rows, 512)
 

time: 89.3 us -> 81 us (0.907)
  waiting for transfers between devices: 51.6 us -> 41.2 us
  starting transfers between devices: 3.43 us -> 7.13 us
  matrix products: 15.2 us -> 14.1 us
    all_gather x1 -> x0, waiting for transfers between devices: 28 us -> none  [attend(): shards = lax.all_gather(pair_shard[0], 'ctx', axis=0, tiled=True)]
    ppermute x0 -> x3, waiting for transfers between devices: none -> 20.2 us  [attend(): lax.ppermute(ring[-1], 'ctx', [(dev, (dev + 1) % 4) for dev in range(4)])]
    ppermute x0 -> x3, starting transfers between devices: none -> 3.81 us  [attend(): lax.ppermute(ring[-1], 'ctx', [(dev, (dev + 1) % 4) for dev in range(4)])]
    ppermute x1, waiting for transfers between devices: 13.8 us -> 11.1 us  [from_behind(): lax.ppermute(value, axis, [(i, (i + by) % size) for i in range(size)])]
    dot_general x1, matrix products: 2.02 us -> 0.92 us  [update(): jnp.einsum('rhgd,khd->hgrk', query_heads, key_block[:, :, :head_dim], pre...]
    unnamed x6 -> x13, local copies, waits for them, and re-layouts: 3.29 us -> 2.8 us
  transfers between devices with their start and end apart: 3 -> 5, of which waited for: 3 -> 5; matrix products, arithmetic and copies ran while one was open for 2% -> 3% of each run, Pallas kernels for 0% -> 0%
where the time goes in v1:
time: 81 us; the launch traced here: 80.9 us
  waiting for transfers between devices  41.2 us (51%)
  matrix products  14.1 us (17%)
  between operations  13.5 us (17%)
  starting transfers between devices  7.13 us (9%)
  local copies, waits for them, and re-layouts  3.15 us (4%)
  other arithmetic  1.76 us (2%)
    ppermute x3, waiting for transfers between devices, attend(): lax.ppermute(ring[-1], 'ctx', [(dev, (dev + 1) % 4) for dev in range(4)])  20.2 us
    dot_general x1, matrix products, local(): jnp.dot(attended.reshape(rows_here, -1), out_proj[0].reshape(-1, out_proj...  11.7 us
    ppermute x1, waiting for transfers between devices, from_behind(): lax.ppermute(value, axis, [(i, (i + by) % size) for i in range(size)])  11.1 us
    reduce_scatter x1, waiting for transfers between devices, local(): lax.psum_scatter(partial_sum.astype(jnp.bfloat16), 'tp', scatter_dimensio...  9.8 us
    ppermute x3, starting transfers between devices, attend(): lax.ppermute(ring[-1], 'ctx', [(dev, (dev + 1) % 4) for dev in range(4)])  3.81 us
    ppermute x1, starting transfers between devices, from_behind(): lax.ppermute(value, axis, [(i, (i + by) % size) for i in range(size)])  3.33 us
    unnamed x13, local copies, waits for them, and re-layouts  2.8 us
  transfers between devices with their start and end apart: 5, of which 5 were waited for; matrix products, arithmetic and copies ran while one was open for 3% of the time, Pallas kernels for 0%

profile of v1, /device:TPU:0, one launch (start us, length us, event | category | flops | bytes accessed | tf_op | source)
XLA Modules:
  0.0 80.9 jit_solution(18145054620688694647)
XLA Ops:
  6.5 0.0 copy-start
  6.5 0.0 copy-start.1
  6.5 0.0 reduce-scatter.2.cloned.1.call-start
  6.5 1.0 %copy.33 = bf16[1,128,4,256]{3,1,2,0:T(8,128)(2,1)S(1)} copy(bf16[1,128,4,256]{3,2,1,0:T(4,128)(2,1)} %param.5) | data formatting | bytes 524288 | tf_op args[1]
  7.6 3.0 %collective-permute-start = (bf16[128,4,256]{2,0,1:T(8,128)(2,1)S(1)}, bf16[128,4,256]{2,0,1:T(8,128)(2,1)S(1)}, u32[]{:S(2)}, u32[]{:S(2)}) collective-permute-start(bf16[128,4,256]{2,0,1:T(8,128)(2,1)S(1)} %bitcast.71), channel_id=1, source_target_pairs={{0,2},{2,4},{4,6},{6,0},{1,3},{3,5},{5,7},{7,1},{8,10},{10,12},{12... | collective-permute-start | bytes 786440 | tf_op jit(solution)/shard_map/ppermute | solution.py:67
  10.6 7.3 %collective-permute-done = bf16[128,4,256]{2,0,1:T(8,128)(2,1)S(1)} collective-permute-done((bf16[128,4,256]{2,0,1:T(8,128)(2,1)S(1)}, bf16[128,4,256]{2,0,1:T(8,128)(2,1)S(1)}, u32[]{:S(2)}, u32[]{:S(2)}) %collective-permute-start) | collective-permute-done | bytes 262176 | tf_op jit(solution)/shard_map/ppermute | solution.py:67
  17.9 0.8 collective-permute-start.1
  18.7 0.0 copy-done
  18.7 0.2 reduce-window.8
  18.9 0.1 convert_reduce_fusion.1
  18.9 7.3 %collective-permute-done.1 = bf16[128,4,256]{2,0,1:T(8,128)(2,1)S(1)} collective-permute-done((bf16[128,4,256]{2,0,1:T(8,128)(2,1)S(1)}, bf16[128,4,256]{2,0,1:T(8,128)(2,1)S(1)}, u32[]{:S(2)}, u32[]{:S(2)}) %collective-permute-start.1) | collective-permute-done | bytes 262176 | tf_op jit(solution)/shard_map/ppermute | solution.py:67
  26.2 0.0 collective-permute-start.2
  26.2 0.1 convert_reduce_fusion
  26.3 1.6 %copy.17 = bf16[1,128,4,640]{1,3,2,0:T(8,128)(2,1)S(1)} copy(bf16[1,128,4,640]{3,2,1,0:T(4,128)(2,1)} %param.4) | data formatting | bytes 1310720 | tf_op args[0]
  27.9 0.1 fusion.24
  28.1 5.7 %collective-permute-done.2 = bf16[128,4,256]{2,0,1:T(8,128)(2,1)S(1)} collective-permute-done((bf16[128,4,256]{2,0,1:T(8,128)(2,1)S(1)}, bf16[128,4,256]{2,0,1:T(8,128)(2,1)S(1)}, u32[]{:S(2)}, u32[]{:S(2)}) %collective-permute-start.2) | collective-permute-done | bytes 262176 | tf_op jit(solution)/shard_map/ppermute | solution.py:67
  33.8 0.0 copy-done.1
  34.0 0.9 %fusion.8 = (f32[4,5,128]{2,1,0:T(8,128)S(1)}, f32[4,512,128,5]{2,1,3,0:T(8,128)S(1)}) fusion(pred[128,512]{0,1:T(8,128)(4,1)S(1)} %fusion.24, bf16[128,4,5,128]{0,3,2,1:T(8,128)(2,1)S(1)} %bitcast.69, bf16[1024,4,256]{2,0,1:T(8,128)(2,1)S(1)} %constant_dynamic-update-slice_fusion, s32[]{:T(128)S(6)} %select_n.29), kind=kOutput, calls=%fused_computation.6 | convolution fusion | flops 339473920 | bytes 6498308 | tf_op jit(solution)/shard_map/while/body/eval_jaxpr/rhgd,khd->hgrk/dot_general | solution.py:38
  34.9 1.2 %fusion.9 = f32[4,5,128]{2,1,0:T(8,128)S(1)} fusion(f32[4,512,128,5]{2,1,3,0:T(8,128)S(1)} %get-tuple-element.26, f32[4,5,128]{2,1,0:T(8,128)S(1)} %get-tuple-element.24, pred[128,512]{0,1:T(8,128)(4,1)S(1)} %fusion.24), kind=kLoop, calls=%fused_computation.7 | loop fusion | flops 6551040 | bytes 5328896 | tf_op jit(solution)/shard_map/while/body/eval_jaxpr/reduce_sum | solution.py:50
  36.2 1.5 %divide_convert_fusion = bf16[128,4,5,128]{0,3,2,1:T(8,128)(2,1)S(1)} fusion(f32[4,512,128,5]{2,1,3,0:T(8,128)S(1)} %get-tuple-element.26, f32[4,5,128]{2,1,0:T(8,128)S(1)} %get-tuple-element.24, pred[128,512]{0,1:T(8,128)(4,1)S(1)} %fusion.24, f32[128,4,5]{0,2,1:T(8,128)S(1)} %bitcast_add_fusion, f32[128,4,5]{0,2,1:T(8,128)S(1)} %get-tuple-element.23, ...), kind=kOutput, calls=%fused_computation.13 | convolution fusion | flops 343080960 | bytes 6537224 | tf_op jit(solution)/shard_map/while/body/eval_jaxpr/hgrk,khd->hgrd/dot_general | solution.py:51
  37.7 0.3 copy.21
  38.0 3.3 %collective-permute-start.3 = (bf16[1,128,4,640]{3,1,2,0:T(8,128)(2,1)S(1)}, bf16[1,128,4,640]{3,1,2,0:T(8,128)(2,1)S(1)}, u32[]{:S(2)}, u32[]{:S(2)}) collective-permute-start(bf16[1,128,4,640]{3,1,2,0:T(8,128)(2,1)S(1)} %copy.21), channel_id=1, source_target_pairs={{0,24},{8,0},{16,8},{24,16},{1,25},{9,1},{17,9},{25,17},{2,26},{10... | collective-permute-start | bytes 1966088 | tf_op jit(solution)/shard_map/ppermute | solution.py:10
  41.4 11.1 %collective-permute-done.3 = bf16[1,128,4,640]{3,1,2,0:T(8,128)(2,1)S(1)} collective-permute-done((bf16[1,128,4,640]{3,1,2,0:T(8,128)(2,1)S(1)}, bf16[1,128,4,640]{3,1,2,0:T(8,128)(2,1)S(1)}, u32[]{:S(2)}, u32[]{:S(2)}) %collective-permute-start.3) | collective-permute-done | bytes 655392 | tf_op jit(solution)/shard_map/ppermute | solution.py:10
  52.5 11.7 %fusion.5 = bf16[128,5120]{1,0:T(8,128)(2,1)} fusion(bf16[1,4,640,5120]{3,2,1,0:T(8,128)(2,1)} %param.6, bf16[1,128,4,640]{3,1,2,0:T(8,128)(2,1)S(1)} %collective-permute-done.3), kind=kOutput, calls=%fused_computation.3 | convolution fusion | flops 3356098560 | bytes 28180480 | tf_op jit(solution)/shard_map/dot_general | solution.py:91
  64.2 0.0 reduce-scatter.2.cloned.1.call-update
  64.3 9.8 %reduce-scatter.2.cloned.1.call-done = bf16[128,2560]{1,0:T(8,128)(2,1)} async-done(((bf16[128,5120]{1,0:T(8,128)(2,1)}), bf16[128,2560]{1,0:T(8,128)(2,1)}) %reduce-scatter.2.cloned.1.call-update) | async-done | bytes 655376 | tf_op jit(solution)/shard_map/reduce_scatter | solution.py:96
  (12 shorter events, 0.2 us)
Async XLA Ops:
  6.5 12.1 %copy-start = (s32[4,4]{1,0:T(4,128)S(1)}, s32[4,4]{1,0:T(4,128)}, u32[]{:S(2)}) copy-start(s32[4,4]{1,0:T(4,128)} %param.7) | copy-start | bytes 196
  6.5 27.3 %copy-start.1 = (bf16[1,128,4,256]{3,2,1,0:T(4,128)(2,1)S(1)}, bf16[1,128,4,256]{3,2,1,0:T(4,128)(2,1)}, u32[]{:S(2)}) copy-start(bf16[1,128,4,256]{3,2,1,0:T(4,128)(2,1)} %param.5) | copy-start | bytes 786436
  6.5 67.5 %reduce-scatter.2.cloned.1.call-start = ((), (), s32[]{:S(2)}) async-start(), calls=%async_computation.1 | async-start | bytes 1966080 | tf_op jit(solution)/shard_map/reduce_scatter | solution.py:96
  7.6 10.3 %collective-permute-start = (bf16[128,4,256]{2,0,1:T(8,128)(2,1)S(1)}, bf16[128,4,256]{2,0,1:T(8,128)(2,1)S(1)}, u32[]{:S(2)}, u32[]{:S(2)}) collective-permute-start(bf16[128,4,256]{2,0,1:T(8,128)(2,1)S(1)} %bitcast.71), channel_id=1, source_target_pairs={{0,2},{2,4},{4,6},{6,0},{1,3},{3,5},{5,7},{7,1},{8,10},{10,12},{12... | collective-permute-start | bytes 786440 | tf_op jit(solution)/shard_map/ppermute | solution.py:67
  17.9 8.4 %collective-permute-start.1 = (bf16[128,4,256]{2,0,1:T(8,128)(2,1)S(1)}, bf16[128,4,256]{2,0,1:T(8,128)(2,1)S(1)}, u32[]{:S(2)}, u32[]{:S(2)}) collective-permute-start(bf16[128,4,256]{2,0,1:T(8,128)(2,1)S(1)} %collective-permute-done), channel_id=1, source_target_pairs={{0,2},{2,4},{4,6},{6,0},{1,3},{3,5},{5,7},{7,1},{8,10},{10,12},{12... | collective-permute-start | bytes 786440 | tf_op jit(solution)/shard_map/ppermute | solution.py:67
  26.2 7.5 %collective-permute-start.2 = (bf16[128,4,256]{2,0,1:T(8,128)(2,1)S(1)}, bf16[128,4,256]{2,0,1:T(8,128)(2,1)S(1)}, u32[]{:S(2)}, u32[]{:S(2)}) collective-permute-start(bf16[128,4,256]{2,0,1:T(8,128)(2,1)S(1)} %collective-permute-done.1), channel_id=1, source_target_pairs={{0,2},{2,4},{4,6},{6,0},{1,3},{3,5},{5,7},{7,1},{8,10},{10,12},{12... | collective-permute-start | bytes 786440 | tf_op jit(solution)/shard_map/ppermute | solution.py:67
  38.0 14.5 %collective-permute-start.3 = (bf16[1,128,4,640]{3,1,2,0:T(8,128)(2,1)S(1)}, bf16[1,128,4,640]{3,1,2,0:T(8,128)(2,1)S(1)}, u32[]{:S(2)}, u32[]{:S(2)}) collective-permute-start(bf16[1,128,4,640]{3,1,2,0:T(8,128)(2,1)S(1)} %copy.21), channel_id=1, source_target_pairs={{0,24},{8,0},{16,8},{24,16},{1,25},{9,1},{17,9},{25,17},{2,26},{10... | collective-permute-start | bytes 1966088 | tf_op jit(solution)/shard_map/ppermute | solution.py:10
Sparse Core Ops, SparseCore 0:
  64.4 9.6 reduce-scatter.1
